TPU v7x, 32 devices: a whole 2x2x4 slice. The times are simulated.
32 devices in a mesh: grp: 2 (over y), mem: 8 (over z, x), slab: 2 (over core).
Axes of the slice: x: 2, y: 2, z: 4, core: 2. Of those that a mesh axis runs over, the one named last changes fastest.
Arguments:
- parameter_field: float32 [32, 32, 32, 256], P(('grp', 'mem'), 'slab'), parts along dimension 0, may hold values from -5 to 5
- initial_tracer: float32 [64, 32, 256], P(('grp', 'slab')), parts along dimension 0, may hold values from -1 to 1
- observed: float32 [8192], P(('grp', 'slab')), parts along dimension 0, may hold values from -3 to 3
- observation_variance: float32 [8192], P(('grp', 'slab')), parts along dimension 0, may hold values from 0.25 to 2.5
- observation_index: int32 [8192], P(('grp', 'slab')), parts along dimension 0, may hold values from 0 to 262143, as said below
- noise: float32 [32, 16], P('grp'), parts along dimension 0, may hold values from -6 to 6
Outputs:
- new_field: float32 [32, 32, 32, 256], P(('grp', 'mem'), 'slab'), parts along dimension 0
- predicted: float32 [32, 4096], P(('grp', 'mem'), 'slab'), parts along dimension 0
- mixing: float32 [32, 16], P(('grp', 'mem')), parts along dimension 0
There are 2 independent parts, one for each index of `grp`. A program takes and returns all parts, laid end to end along the dimension named above; each array names one. Nothing has to cross between parts.
Inputs may be any that keep to these rules, and one draw needn't show every extreme that they name: `observation_index`: observation i names a flattened cell whose x lies in x-slab i // 2048, that is from (i // 2048) * 16 to (i // 2048) * 16 + 15; cells may repeat.
All inputs are finite; a program needn't handle non-finite values.
Results may differ from a plain program's by a relative error of at most 0.00011.
Values sent between devices are 32-bit elements; how exact they have to be, the bound alone decides.
No kernel may reach another device: no remote copies, remote signals or barrier semaphores. Data moves between devices by JAX's collectives and lax.ppermute only.
A program may use at most 192 MiB of HBM per device.

v0:
```python
import jax
import jax.numpy as jnp
from jax import lax
from jax.sharding import PartitionSpec as P

STEPS = 3
ADVECT_SPEED = 0.1
KAPPA_BASE = 0.07
KAPPA_SWING = 0.05
STEP_SCALE = 0.02
PRIOR_VARIANCE = 0.02
EPSILON = 1e-06


def padded(block, sides, width):
    for axis, dim in sides:
        count = lax.axis_size(axis)
        forward = [(i, i + 1) for i in range(count - 1)]
        forward.append((count - 1, 0))
        backward = [(target, source) for source, target in forward]
        low = lax.ppermute(
            lax.slice_in_dim(block, block.shape[dim] - width, None, axis=dim), axis, forward
        )
        high = lax.ppermute(lax.slice_in_dim(block, 0, width, axis=dim), axis, backward)
        block = jnp.concatenate([low, block, high], axis=dim)
    return block


def advance(extended, diffusivity):
    center = extended[:, 1:-1]
    upper_level = jnp.concatenate([center[:, :, 1:], center[:, :, -1:]], axis=2)
    lower_level = jnp.concatenate([center[:, :, :1], center[:, :, :-1]], axis=2)
    laplace = (
        extended[:, 2:]
        + extended[:, :-2]
        + upper_level
        + lower_level
        + jnp.roll(center, 1, axis=3)
        + jnp.roll(center, -1, axis=3)
        - 6.0 * center
    )
    fluxes = 0.5 * ADVECT_SPEED * extended * extended
    wave_speed = ADVECT_SPEED * jnp.maximum(jnp.abs(extended[:, :-1]), jnp.abs(extended[:, 1:]))
    face_flux = 0.5 * (fluxes[:, :-1] + fluxes[:, 1:]) - 0.5 * wave_speed * (
        extended[:, 1:] - extended[:, :-1]
    )
    return center + diffusivity * laplace - (face_flux[:, 1:] - face_flux[:, :-1])


def misfit_products(values, observed, variance):
    member_mean = jnp.mean(values, axis=0, keepdims=True)
    spread_obs = values - member_mean
    weighted = (values - observed[None]) / variance[None]
    return jnp.einsum(
        "ko,jo->kj",
        spread_obs,
        weighted,
        precision=lax.Precision.HIGHEST,
        preferred_element_type=jnp.float32,
    )


def per_device(
    parameter_field, initial_tracer, observed, observation_variance, observation_index, noise
):
    members_here, slab_width, levels, columns = parameter_field.shape
    ensemble = noise.shape[0]
    tracer = padded(initial_tracer[None], (("slab", 1),), STEPS)
    param_rim = padded(parameter_field, (("slab", 1),), STEPS - 1)
    diffusivity_rim = KAPPA_BASE + KAPPA_SWING * jnp.tanh(param_rim)
    for step_number in range(STEPS):
        margin = STEPS - 1 - step_number
        offset = STEPS - 1 - margin
        diffusivity_now = diffusivity_rim[:, offset : offset + slab_width + 2 * margin]
        tracer = advance(tracer, diffusivity_now)
    cell_count = slab_width * levels * columns
    slab_number = lax.axis_index("slab")
    flat_tracer = tracer.reshape(members_here, cell_count)
    local_index = observation_index - slab_number * cell_count
    predicted = jnp.take(flat_tracer, local_index, axis=1)
    total_cells = cell_count * lax.axis_size("slab")
    flat_param = parameter_field.reshape(members_here, cell_count)
    spread = lax.all_to_all(flat_param, "mem", split_axis=1, concat_axis=0, tiled=True)
    center_mean = jnp.mean(spread, axis=0, keepdims=True)
    deviation = spread - center_mean
    prior_part = jnp.einsum(
        "kc,jc->kj",
        deviation,
        spread,
        precision=lax.Precision.HIGHEST,
        preferred_element_type=jnp.float32,
    )
    gathered = lax.all_gather(predicted, "mem", axis=0, tiled=True)
    data_part = misfit_products(gathered, observed, observation_variance)
    data_total = lax.psum(data_part, "slab")
    prior_total = lax.psum(prior_part, ("mem", "slab"))
    data_gram = data_total / ensemble
    prior_gram = prior_total / (ensemble * PRIOR_VARIANCE * total_cells)
    step_size = STEP_SCALE / jnp.sqrt(jnp.mean(data_gram * data_gram) + EPSILON)
    mixing = -step_size * (data_gram + prior_gram) + jnp.sqrt(2.0 * step_size / ensemble) * noise
    updated = spread + jnp.einsum(
        "kj,kc->jc",
        mixing,
        deviation,
        precision=lax.Precision.HIGHEST,
        preferred_element_type=jnp.float32,
    )
    returned = lax.all_to_all(updated, "mem", split_axis=0, concat_axis=1, tiled=True)
    new_field = returned.reshape(members_here, slab_width, levels, columns)
    mixing_rows = lax.dynamic_slice_in_dim(
        mixing, lax.axis_index("mem") * members_here, members_here, 0
    )
    return (new_field, predicted, mixing_rows)


def solution(mesh):
    in_specs = (
        P(("grp", "mem"), "slab", None, None),
        P(("grp", "slab"), None, None),
        P(("grp", "slab")),
        P(("grp", "slab")),
        P(("grp", "slab")),
        P("grp", None),
    )
    out_specs = (
        P(("grp", "mem"), "slab", None, None),
        P(("grp", "mem"), "slab"),
        P(("grp", "mem"), None),
    )
    return jax.shard_map(
        per_device, mesh=mesh, in_specs=in_specs, out_specs=out_specs, check_vma=False
    )
```

profile of v0, /device:TPU:0, one launch (start us, length us, event | category | flops | bytes accessed | tf_op | source)
XLA Modules:
  0.0 181.7 jit_solution(15744411781428949287)
XLA Ops:
  0.6 1.0 fusion.55
  1.6 0.6 collective-permute-start
  2.2 1.0 fusion.50
  3.2 0.5 collective-permute-start.2
  3.8 1.4 all_to_all.26
  5.2 1.8 copy.18
  7.0 7.4 %all-to-all-start = ((f32[2,8,16384]{2,0,1:T(2,128)}), f32[2,8,16384]{2,0,1:T(2,128)S(1)}, u32[]{:S(2)}, u32[]{:S(2)}) async-start(f32[2,8,16384]{2,0,1:T(2,128)} %copy.18), calls=%async_computation | async-start | bytes 2097152 | tf_op jit(solution)/shard_map/all_to_all | solution.py:83
  15.3 0.5 slice_bitcast_fusion
  15.9 0.6 copy-done
  16.5 0.6 multiply_multiply_fusion
  17.5 0.4 fusion.45
  18.5 1.3 multiply_multiply_fusion.1
  21.1 1.1 fusion.14
  22.2 32.5 %copy.19 = f32[2,16,32,256]{0,3,2,1:T(8,128)} copy(f32[2,16,32,256]{3,2,1,0:T(8,128)S(1)} %fusion.14) | data formatting | bytes 2097152 | tf_op jit(solution)/shard_map/sub | solution.py:47
  54.7 20.5 %gather_fusion = f32[2048,2]{1,0:T(8,128)S(1)} fusion(f32[2,131072]{0,1:T(8,128)} %bitcast.5, s32[2048]{0:T(1024)S(1)} %fusion.40), kind=kCustom, calls=%fused_computation | custom fusion | bytes 40960 | tf_op jit(solution)/shard_map/jit(_take)/gather | solution.py:80
  75.2 1.3 select_bitcast_fusion.1
  76.9 31.1 %all-gather = f32[8,2,2048]{2,1,0:T(2,128)S(1)} all-gather(f32[1,2,2048]{2,1,0:T(2,128)S(1)} %copy.20), channel_id=1, replica_groups=mesh['grp'=2,'mem'=8,'slab'=2] {'mem'}, dimensions={0}, use_global_device_ids=true | all-gather | bytes 147456 | tf_op jit(solution)/shard_map/all_gather | solution.py:93
  108.5 2.5 %psum.14 = f32[16,16]{1,0:T(8,128)S(1)} all-reduce(f32[16,16]{1,0:T(8,128)S(1)} %fusion.33), channel_id=1, replica_groups=mesh['grp'=2,'mem'=8,'slab'=2] {'slab'}, use_global_device_ids=true, to_apply=%region_1.2 | all-reduce | flops 256 | bytes 2048 | tf_op jit(solution)/shard_map/psum | solution.py:95
  111.0 0.6 multiply_reduce_fusion
  112.4 0.4 reduce_sum.29
  113.2 0.7 sub.114
  113.9 0.7 all_to_all.29
  114.6 1.4 fusion.56
  116.1 33.9 %psum.15 = f32[16,16]{1,0:T(8,128)S(1)} all-reduce(f32[16,16]{1,0:T(8,128)S(1)} %fusion.56), channel_id=1, replica_groups=mesh['grp'=2,'mem'=8,'slab'=2] {'mem','slab'}, use_global_device_ids=true, to_apply=%region_4.5 | all-reduce | flops 256 | bytes 2048 | tf_op jit(solution)/shard_map/psum | solution.py:96
  149.9 1.0 convolution_add_fusion
  151.0 1.6 all_to_all.30
  152.6 3.7 %all-to-all-start.1 = ((f32[8,2,16384]{2,1,0:T(2,128)}), f32[8,2,16384]{2,1,0:T(2,128)S(1)}, u32[]{:S(2)}, u32[]{:S(2)}) async-start(f32[8,2,16384]{2,1,0:T(2,128)} %all_to_all.30), calls=%async_computation.1 | async-start | bytes 2097152 | tf_op jit(solution)/shard_map/all_to_all | solution.py:108
  156.3 0.9 copy.22
  157.2 0.6 constant_dynamic-slice_fusion
  157.8 22.2 %all-to-all-done.1 = f32[8,2,16384]{2,1,0:T(2,128)S(1)} async-done(((f32[8,2,16384]{2,1,0:T(2,128)}), f32[8,2,16384]{2,1,0:T(2,128)S(1)}, u32[]{:S(2)}, u32[]{:S(2)}) %all-to-all-start.1) | async-done | bytes 1048608 | tf_op jit(solution)/shard_map/all_to_all | solution.py:108
  180.0 0.6 copy.21
  180.6 1.1 reshape.131
  (45 shorter events, 4.3 us)
Async XLA Ops:
  1.6 12.8 %collective-permute-start = (f32[1,3,32,256]{3,2,1,0:T(8,128)S(1)}, f32[1,3,32,256]{3,2,1,0:T(8,128)S(1)}, u32[]{:S(2)}, u32[]{:S(2)}) collective-permute-start(f32[1,3,32,256]{3,2,1,0:T(8,128)S(1)} %get-tuple-element.49), channel_id=1, source_target_pairs={{0,1},{1,0},{2,3},{3,2},{4,5},{5,4},{6,7},{7,6},{8,9},{9,8},{10,11... | collective-permute-start | bytes 294920 | tf_op jit(solution)/shard_map/ppermute | solution.py:21
  2.1 12.3 %collective-permute-start.1 = (f32[1,3,32,256]{3,2,1,0:T(8,128)S(1)}, f32[1,3,32,256]{3,2,1,0:T(8,128)S(1)}, u32[]{:S(2)}, u32[]{:S(2)}) collective-permute-start(f32[1,3,32,256]{3,2,1,0:T(8,128)S(1)} %get-tuple-element.50), channel_id=1, source_target_pairs={{1,0},{0,1},{3,2},{2,3},{5,4},{4,5},{7,6},{6,7},{9,8},{8,9},{11,10... | collective-permute-start | bytes 294920 | tf_op jit(solution)/shard_map/ppermute | solution.py:24
  3.2 12.7 %collective-permute-start.2 = (f32[2,2,32,256]{3,2,1,0:T(8,128)S(1)}, f32[2,2,32,256]{3,2,1,0:T(8,128)S(1)}, u32[]{:S(2)}, u32[]{:S(2)}) collective-permute-start(f32[2,2,32,256]{3,2,1,0:T(8,128)S(1)} %get-tuple-element.35), channel_id=1, source_target_pairs={{0,1},{1,0},{2,3},{3,2},{4,5},{5,4},{6,7},{7,6},{8,9},{9,8},{10,11... | collective-permute-start | bytes 393224 | tf_op jit(solution)/shard_map/ppermute | solution.py:21
  3.7 12.2 %collective-permute-start.3 = (f32[2,2,32,256]{3,2,1,0:T(8,128)S(1)}, f32[2,2,32,256]{3,2,1,0:T(8,128)S(1)}, u32[]{:S(2)}, u32[]{:S(2)}) collective-permute-start(f32[2,2,32,256]{3,2,1,0:T(8,128)S(1)} %get-tuple-element.36), channel_id=1, source_target_pairs={{1,0},{0,1},{3,2},{2,3},{5,4},{4,5},{7,6},{6,7},{9,8},{8,9},{11,10... | collective-permute-start | bytes 393224 | tf_op jit(solution)/shard_map/ppermute | solution.py:24
  7.0 7.4 %copy-start.3 = (s32[2048]{0:T(1024)S(1)}, s32[2048]{0:T(1024)}, u32[]{:S(2)}) copy-start(s32[2048]{0:T(1024)} %param.10) | copy-start | bytes 24580
  7.0 7.4 %copy-start.2 = (f32[16,32,256]{2,1,0:T(8,128)S(1)}, f32[16,32,256]{2,1,0:T(8,128)}, u32[]{:S(2)}) copy-start(f32[16,32,256]{2,1,0:T(8,128)} %param.7) | copy-start | bytes 1572868
  7.0 105.3 %all-to-all-start = ((f32[2,8,16384]{2,0,1:T(2,128)}), f32[2,8,16384]{2,0,1:T(2,128)S(1)}, u32[]{:S(2)}, u32[]{:S(2)}) async-start(f32[2,8,16384]{2,0,1:T(2,128)} %copy.18), calls=%async_computation | async-start | bytes 2097152 | tf_op jit(solution)/shard_map/all_to_all | solution.py:83
  15.3 1.2 copy-start
  76.5 31.7 %copy-start.5 = (f32[2048]{0:T(1024)S(1)}, f32[2048]{0:T(1024)}, u32[]{:S(2)}) copy-start(f32[2048]{0:T(1024)} %param.9) | copy-start | bytes 24580
  76.5 31.7 %copy-start.6 = (f32[2048]{0:T(1024)S(1)}, f32[2048]{0:T(1024)}, u32[]{:S(2)}) copy-start(f32[2048]{0:T(1024)} %param.8) | copy-start | bytes 24580
  114.6 35.3 %copy-start.4 = (f32[16,16]{1,0:T(8,128)S(1)}, f32[16,16]{1,0:T(8,128)}, u32[]{:S(2)}) copy-start(f32[16,16]{1,0:T(8,128)} %param.11) | copy-start | bytes 3076
  152.6 3.7 %copy-start.1 = (f32[2,2048]{0,1:T(8,128)S(1)}, f32[2,2048]{0,1:T(8,128)}, u32[]{:S(2)}) copy-start(f32[2,2048]{0,1:T(8,128)} %get-tuple-element.33) | copy-start | bytes 49156
  152.6 27.4 %all-to-all-start.1 = ((f32[8,2,16384]{2,1,0:T(2,128)}), f32[8,2,16384]{2,1,0:T(2,128)S(1)}, u32[]{:S(2)}, u32[]{:S(2)}) async-start(f32[8,2,16384]{2,1,0:T(2,128)} %all_to_all.30), calls=%async_computation.1 | async-start | bytes 2097152 | tf_op jit(solution)/shard_map/all_to_all | solution.py:108
where the time goes:
time: 182 us
  local copies, waits for them, and re-layouts  67.9 us (37%)
  blocking collectives  67.5 us (37%)
  waiting for transfers between devices  22.2 us (12%)
  starting transfers between devices  12.3 us (7%)
  other arithmetic  7.34 us (4%)
  matrix products  2.72 us (1%)
    psum x1, blocking collectives, per_device(): prior_total = lax.psum(prior_part, ('mem', 'slab'))  33.9 us
    sub x1, local copies, waits for them, and re-layouts, advance(): center + diffusivity * laplace - (face_flux[:, 1:] - face_flux[:, :-1])  32.5 us
    all_gather x1, blocking collectives, per_device(): gathered = lax.all_gather(predicted, 'mem', axis=0, tiled=True)  31.1 us
    all_to_all x1, waiting for transfers between devices, per_device(): lax.all_to_all(updated, 'mem', split_axis=0, concat_axis=1, tiled=True)  22.2 us
    gather x1, local copies, waits for them, and re-layouts, per_device(): predicted = jnp.take(flat_tracer, local_index, axis=1)  20.5 us
    all_to_all x1, starting transfers between devices, per_device(): lax.all_to_all(flat_param, 'mem', split_axis=1, concat_axis=0, tiled=True)  7.35 us
    all_to_all x3, local copies, waits for them, and re-layouts, per_device(): lax.all_to_all(flat_param, 'mem', split_axis=1, concat_axis=0, tiled=True)  3.92 us
    all_to_all x1, starting transfers between devices, per_device(): lax.all_to_all(updated, 'mem', split_axis=0, concat_axis=1, tiled=True)  3.69 us
  transfers between devices with their start and end apart: 6, of which 1 were waited for; matrix products, arithmetic and copies ran while one was open for 37% of the time, Pallas kernels for 0%

commit v1 on v0

--- a/solution.py
+++ b/solution.py
@@ -90,7 +90,12 @@
         precision=lax.Precision.HIGHEST,
         preferred_element_type=jnp.float32,
     )
-    gathered = lax.all_gather(predicted, "mem", axis=0, tiled=True)
+    ring = [predicted]
+    for hop in range(7):
+        ring.append(lax.ppermute(ring[-1], "mem", [(dev, (dev + 1) % 8) for dev in range(8)]))
+    gathered = jnp.roll(
+        jnp.concatenate(ring[::-1], axis=0), (lax.axis_index("mem") + 1) * ring[0].shape[0], axis=0
+    )
     data_part = misfit_products(gathered, observed, observation_variance)
     data_total = lax.psum(data_part, "slab")
     prior_total = lax.psum(prior_part, ("mem", "slab"))

time: 182 us -> 194 us (1.066)
  waiting for transfers between devices: 22.2 us -> 68.3 us
  blocking collectives: 67.5 us -> 32.7 us
    ppermute x0 -> x7, waiting for transfers between devices: none -> 43 us  [per_device(): lax.ppermute(ring[-1], 'mem', [(dev, (dev + 1) % 8) for dev in range(8)])]
    all_gather x1 -> x0, blocking collectives: 31.1 us -> none  [per_device(): gathered = lax.all_gather(predicted, 'mem', axis=0, tiled=True)]
    psum x1, blocking collectives: 33.9 us -> 30.2 us  [per_device(): prior_total = lax.psum(prior_part, ('mem', 'slab'))]
    all_to_all x1, waiting for transfers between devices: 22.2 us -> 25.2 us  [per_device(): lax.all_to_all(updated, 'mem', split_axis=0, concat_axis=1, tiled=True)]
    ppermute x0 -> x7, starting transfers between devices: none -> 2.06 us  [per_device(): lax.ppermute(ring[-1], 'mem', [(dev, (dev + 1) % 8) for dev in range(8)])]
  transfers between devices with their start and end apart: 6 -> 13, of which waited for: 1 -> 8; matrix products, arithmetic and copies ran while one was open for 37% -> 34% of each run, Pallas kernels for 0% -> 0%
where the time goes in v1:
time: 194 us; the launch traced here: 193 us
  waiting for transfers between devices  68.3 us (35%)
  local copies, waits for them, and re-layouts  67.1 us (35%)
  blocking collectives  32.7 us (17%)
  starting transfers between devices  14.2 us (7%)
  other arithmetic  6.34 us (3%)
  matrix products  2.73 us (1%)
    ppermute x7, waiting for transfers between devices, per_device(): lax.ppermute(ring[-1], 'mem', [(dev, (dev + 1) % 8) for dev in range(8)])  43 us
    sub x1, local copies, waits for them, and re-layouts, advance(): center + diffusivity * laplace - (face_flux[:, 1:] - face_flux[:, :-1])  32.5 us
    psum x1, blocking collectives, per_device(): prior_total = lax.psum(prior_part, ('mem', 'slab'))  30.2 us
    all_to_all x1, waiting for transfers between devices, per_device(): lax.all_to_all(updated, 'mem', split_axis=0, concat_axis=1, tiled=True)  25.2 us
    gather x1, local copies, waits for them, and re-layouts, per_device(): predicted = jnp.take(flat_tracer, local_index, axis=1)  20.5 us
    all_to_all x1, starting transfers between devices, per_device(): lax.all_to_all(flat_param, 'mem', split_axis=1, concat_axis=0, tiled=True)  7.35 us
    all_to_all x3, local copies, waits for them, and re-layouts, per_device(): lax.all_to_all(flat_param, 'mem', split_axis=1, concat_axis=0, tiled=True)  3.92 us
  transfers between devices with their start and end apart: 13, of which 8 were waited for; matrix products, arithmetic and copies ran while one was open for 34% of the time, Pallas kernels for 0%

profile of v1, /device:TPU:0, one launch (start us, length us, event | category | flops | bytes accessed | tf_op | source)
XLA Modules:
  0.0 193.1 jit_solution(10544465366691864502)
XLA Ops:
  0.6 1.0 fusion.57
  2.2 1.0 fusion.52
  3.8 1.4 all_to_all.26
  5.2 1.8 copy.13
  7.0 7.4 %all-to-all-start = ((f32[2,8,16384]{2,0,1:T(2,128)}), f32[2,8,16384]{2,0,1:T(2,128)S(1)}, u32[]{:S(2)}, u32[]{:S(2)}) async-start(f32[2,8,16384]{2,0,1:T(2,128)} %copy.13), calls=%async_computation | async-start | bytes 2097152 | tf_op jit(solution)/shard_map/all_to_all | solution.py:83
  15.9 0.6 copy-done
  16.5 0.6 multiply_multiply_fusion
  18.5 1.3 multiply_multiply_fusion.1
  21.1 1.1 fusion.14
  22.2 32.5 %copy.14 = f32[2,16,32,256]{0,3,2,1:T(8,128)} copy(f32[2,16,32,256]{3,2,1,0:T(8,128)S(1)} %fusion.14) | data formatting | bytes 2097152 | tf_op jit(solution)/shard_map/sub | solution.py:47
  54.7 20.5 %gather_fusion = f32[2048,2]{1,0:T(8,128)S(1)} fusion(f32[2,131072]{0,1:T(8,128)} %bitcast.5, s32[2048]{0:T(1024)S(1)} %fusion.41), kind=kCustom, calls=%fused_computation | custom fusion | bytes 40960 | tf_op jit(solution)/shard_map/jit(_take)/gather | solution.py:80
  75.9 2.0 %collective-permute-start.4 = (f32[2,2048]{1,0:T(2,128)S(1)}, f32[2,2048]{1,0:T(2,128)S(1)}, u32[]{:S(2)}, u32[]{:S(2)}) collective-permute-start(f32[2,2048]{1,0:T(2,128)S(1)} %copy.15), channel_id=1, source_target_pairs={{0,2},{2,4},{4,6},{6,8},{8,10},{10,12},{12,14},{14,0},{1,3},{3,5},... | collective-permute-start | bytes 49160 | tf_op jit(solution)/shard_map/ppermute | solution.py:95
  77.9 4.4 %collective-permute-done.4 = f32[2,2048]{1,0:T(2,128)S(1)} collective-permute-done((f32[2,2048]{1,0:T(2,128)S(1)}, f32[2,2048]{1,0:T(2,128)S(1)}, u32[]{:S(2)}, u32[]{:S(2)}) %collective-permute-start.4) | collective-permute-done | bytes 16416 | tf_op jit(solution)/shard_map/ppermute | solution.py:95
  82.3 6.4 %collective-permute-done.5 = f32[2,2048]{1,0:T(2,128)S(1)} collective-permute-done((f32[2,2048]{1,0:T(2,128)S(1)}, f32[2,2048]{1,0:T(2,128)S(1)}, u32[]{:S(2)}, u32[]{:S(2)}) %collective-permute-start.5) | collective-permute-done | bytes 16416 | tf_op jit(solution)/shard_map/ppermute | solution.py:95
  88.8 6.4 %collective-permute-done.6 = f32[2,2048]{1,0:T(2,128)S(1)} collective-permute-done((f32[2,2048]{1,0:T(2,128)S(1)}, f32[2,2048]{1,0:T(2,128)S(1)}, u32[]{:S(2)}, u32[]{:S(2)}) %collective-permute-start.6) | collective-permute-done | bytes 16416 | tf_op jit(solution)/shard_map/ppermute | solution.py:95
  95.2 6.4 %collective-permute-done.7 = f32[2,2048]{1,0:T(2,128)S(1)} collective-permute-done((f32[2,2048]{1,0:T(2,128)S(1)}, f32[2,2048]{1,0:T(2,128)S(1)}, u32[]{:S(2)}, u32[]{:S(2)}) %collective-permute-start.7) | collective-permute-done | bytes 16416 | tf_op jit(solution)/shard_map/ppermute | solution.py:95
  101.7 6.4 %collective-permute-done.8 = f32[2,2048]{1,0:T(2,128)S(1)} collective-permute-done((f32[2,2048]{1,0:T(2,128)S(1)}, f32[2,2048]{1,0:T(2,128)S(1)}, u32[]{:S(2)}, u32[]{:S(2)}) %collective-permute-start.8) | collective-permute-done | bytes 16416 | tf_op jit(solution)/shard_map/ppermute | solution.py:95
  108.1 6.4 %collective-permute-done.9 = f32[2,2048]{1,0:T(2,128)S(1)} collective-permute-done((f32[2,2048]{1,0:T(2,128)S(1)}, f32[2,2048]{1,0:T(2,128)S(1)}, u32[]{:S(2)}, u32[]{:S(2)}) %collective-permute-start.9) | collective-permute-done | bytes 16416 | tf_op jit(solution)/shard_map/ppermute | solution.py:95
  114.5 6.4 %collective-permute-done.10 = f32[2,2048]{1,0:T(2,128)S(1)} collective-permute-done((f32[2,2048]{1,0:T(2,128)S(1)}, f32[2,2048]{1,0:T(2,128)S(1)}, u32[]{:S(2)}, u32[]{:S(2)}) %collective-permute-start.10) | collective-permute-done | bytes 16416 | tf_op jit(solution)/shard_map/ppermute | solution.py:95
  121.5 2.5 %psum.14 = f32[16,16]{1,0:T(8,128)S(1)} all-reduce(f32[16,16]{1,0:T(8,128)S(1)} %fusion.33), channel_id=1, replica_groups=mesh['grp'=2,'mem'=8,'slab'=2] {'slab'}, use_global_device_ids=true, to_apply=%region_1.2 | all-reduce | flops 256 | bytes 2048 | tf_op jit(solution)/shard_map/psum | solution.py:100
  124.1 0.6 multiply_reduce_fusion
  126.2 0.7 sub.119
  127.0 0.7 all_to_all.29
  127.7 1.4 fusion.58
  129.1 30.2 %psum.15 = f32[16,16]{1,0:T(8,128)S(1)} all-reduce(f32[16,16]{1,0:T(8,128)S(1)} %fusion.58), channel_id=1, replica_groups=mesh['grp'=2,'mem'=8,'slab'=2] {'mem','slab'}, use_global_device_ids=true, to_apply=%region_4.5 | all-reduce | flops 256 | bytes 2048 | tf_op jit(solution)/shard_map/psum | solution.py:101
  159.3 1.0 convolution_add_fusion
  160.4 1.6 all_to_all.30
  162.0 3.6 %all-to-all-start.1 = ((f32[8,2,16384]{2,1,0:T(2,128)}), f32[8,2,16384]{2,1,0:T(2,128)S(1)}, u32[]{:S(2)}, u32[]{:S(2)}) async-start(f32[8,2,16384]{2,1,0:T(2,128)} %all_to_all.30), calls=%async_computation.1 | async-start | bytes 2097152 | tf_op jit(solution)/shard_map/all_to_all | solution.py:113
  165.5 0.6 constant_dynamic-slice_fusion
  166.1 25.2 %all-to-all-done.1 = f32[8,2,16384]{2,1,0:T(2,128)S(1)} async-done(((f32[8,2,16384]{2,1,0:T(2,128)}), f32[8,2,16384]{2,1,0:T(2,128)S(1)}, u32[]{:S(2)}, u32[]{:S(2)}) %all-to-all-start.1) | async-done | bytes 1048608 | tf_op jit(solution)/shard_map/all_to_all | solution.py:113
  191.3 0.6 copy.18
  191.9 1.1 reshape.131
  (57 shorter events, 7.2 us)
Async XLA Ops:
  1.6 12.8 %collective-permute-start = (f32[1,3,32,256]{3,2,1,0:T(8,128)S(1)}, f32[1,3,32,256]{3,2,1,0:T(8,128)S(1)}, u32[]{:S(2)}, u32[]{:S(2)}) collective-permute-start(f32[1,3,32,256]{3,2,1,0:T(8,128)S(1)} %get-tuple-element.44), channel_id=1, source_target_pairs={{0,1},{1,0},{2,3},{3,2},{4,5},{5,4},{6,7},{7,6},{8,9},{9,8},{10,11... | collective-permute-start | bytes 294920 | tf_op jit(solution)/shard_map/ppermute | solution.py:21
  2.1 12.3 %collective-permute-start.1 = (f32[1,3,32,256]{3,2,1,0:T(8,128)S(1)}, f32[1,3,32,256]{3,2,1,0:T(8,128)S(1)}, u32[]{:S(2)}, u32[]{:S(2)}) collective-permute-start(f32[1,3,32,256]{3,2,1,0:T(8,128)S(1)} %get-tuple-element.45), channel_id=1, source_target_pairs={{1,0},{0,1},{3,2},{2,3},{5,4},{4,5},{7,6},{6,7},{9,8},{8,9},{11,10... | collective-permute-start | bytes 294920 | tf_op jit(solution)/shard_map/ppermute | solution.py:24
  3.2 12.7 %collective-permute-start.2 = (f32[2,2,32,256]{3,2,1,0:T(8,128)S(1)}, f32[2,2,32,256]{3,2,1,0:T(8,128)S(1)}, u32[]{:S(2)}, u32[]{:S(2)}) collective-permute-start(f32[2,2,32,256]{3,2,1,0:T(8,128)S(1)} %get-tuple-element.30), channel_id=1, source_target_pairs={{0,1},{1,0},{2,3},{3,2},{4,5},{5,4},{6,7},{7,6},{8,9},{9,8},{10,11... | collective-permute-start | bytes 393224 | tf_op jit(solution)/shard_map/ppermute | solution.py:21
  3.7 12.2 %collective-permute-start.3 = (f32[2,2,32,256]{3,2,1,0:T(8,128)S(1)}, f32[2,2,32,256]{3,2,1,0:T(8,128)S(1)}, u32[]{:S(2)}, u32[]{:S(2)}) collective-permute-start(f32[2,2,32,256]{3,2,1,0:T(8,128)S(1)} %get-tuple-element.31), channel_id=1, source_target_pairs={{1,0},{0,1},{3,2},{2,3},{5,4},{4,5},{7,6},{6,7},{9,8},{8,9},{11,10... | collective-permute-start | bytes 393224 | tf_op jit(solution)/shard_map/ppermute | solution.py:24
  7.0 7.4 %copy-start.3 = (s32[2048]{0:T(1024)S(1)}, s32[2048]{0:T(1024)}, u32[]{:S(2)}) copy-start(s32[2048]{0:T(1024)} %param.10) | copy-start | bytes 24580
  7.0 7.4 %copy-start.1 = (f32[16,32,256]{2,1,0:T(8,128)S(1)}, f32[16,32,256]{2,1,0:T(8,128)}, u32[]{:S(2)}) copy-start(f32[16,32,256]{2,1,0:T(8,128)} %param.7) | copy-start | bytes 1572868
  7.0 118.4 %all-to-all-start = ((f32[2,8,16384]{2,0,1:T(2,128)}), f32[2,8,16384]{2,0,1:T(2,128)S(1)}, u32[]{:S(2)}, u32[]{:S(2)}) async-start(f32[2,8,16384]{2,0,1:T(2,128)} %copy.13), calls=%async_computation | async-start | bytes 2097152 | tf_op jit(solution)/shard_map/all_to_all | solution.py:83
  15.3 1.2 copy-start
  75.5 45.7 %copy-start.5 = (f32[2048]{0:T(1024)S(1)}, f32[2048]{0:T(1024)}, u32[]{:S(2)}) copy-start(f32[2048]{0:T(1024)} %param.9) | copy-start | bytes 24580
  75.5 45.7 %copy-start.6 = (f32[2048]{0:T(1024)S(1)}, f32[2048]{0:T(1024)}, u32[]{:S(2)}) copy-start(f32[2048]{0:T(1024)} %param.8) | copy-start | bytes 24580
  75.9 49.9 %copy-start.2 = (f32[2,2048]{1,0:T(2,128)}, f32[2,2048]{1,0:T(2,128)S(1)}, u32[]{:S(2)}) copy-start(f32[2,2048]{1,0:T(2,128)S(1)} %copy.15) | copy-start | bytes 49156
  75.9 6.5 %collective-permute-start.4 = (f32[2,2048]{1,0:T(2,128)S(1)}, f32[2,2048]{1,0:T(2,128)S(1)}, u32[]{:S(2)}, u32[]{:S(2)}) collective-permute-start(f32[2,2048]{1,0:T(2,128)S(1)} %copy.15), channel_id=1, source_target_pairs={{0,2},{2,4},{4,6},{6,8},{8,10},{10,12},{12,14},{14,0},{1,3},{3,5},... | collective-permute-start | bytes 49160 | tf_op jit(solution)/shard_map/ppermute | solution.py:95
  82.3 6.4 %collective-permute-start.5 = (f32[2,2048]{1,0:T(2,128)S(1)}, f32[2,2048]{1,0:T(2,128)S(1)}, u32[]{:S(2)}, u32[]{:S(2)}) collective-permute-start(f32[2,2048]{1,0:T(2,128)S(1)} %collective-permute-done.4), channel_id=1, source_target_pairs={{0,2},{2,4},{4,6},{6,8},{8,10},{10,12},{12,14},{14,0},{1,3},{3,5},... | collective-permute-start | bytes 49160 | tf_op jit(solution)/shard_map/ppermute | solution.py:95
  88.8 6.4 %collective-permute-start.6 = (f32[2,2048]{1,0:T(2,128)S(1)}, f32[2,2048]{1,0:T(2,128)S(1)}, u32[]{:S(2)}, u32[]{:S(2)}) collective-permute-start(f32[2,2048]{1,0:T(2,128)S(1)} %collective-permute-done.5), channel_id=1, source_target_pairs={{0,2},{2,4},{4,6},{6,8},{8,10},{10,12},{12,14},{14,0},{1,3},{3,5},... | collective-permute-start | bytes 49160 | tf_op jit(solution)/shard_map/ppermute | solution.py:95
  95.2 6.4 %collective-permute-start.7 = (f32[2,2048]{1,0:T(2,128)S(1)}, f32[2,2048]{1,0:T(2,128)S(1)}, u32[]{:S(2)}, u32[]{:S(2)}) collective-permute-start(f32[2,2048]{1,0:T(2,128)S(1)} %collective-permute-done.6), channel_id=1, source_target_pairs={{0,2},{2,4},{4,6},{6,8},{8,10},{10,12},{12,14},{14,0},{1,3},{3,5},... | collective-permute-start | bytes 49160 | tf_op jit(solution)/shard_map/ppermute | solution.py:95
  101.7 6.4 %collective-permute-start.8 = (f32[2,2048]{1,0:T(2,128)S(1)}, f32[2,2048]{1,0:T(2,128)S(1)}, u32[]{:S(2)}, u32[]{:S(2)}) collective-permute-start(f32[2,2048]{1,0:T(2,128)S(1)} %collective-permute-done.7), channel_id=1, source_target_pairs={{0,2},{2,4},{4,6},{6,8},{8,10},{10,12},{12,14},{14,0},{1,3},{3,5},... | collective-permute-start | bytes 49160 | tf_op jit(solution)/shard_map/ppermute | solution.py:95
  108.1 6.4 %collective-permute-start.9 = (f32[2,2048]{1,0:T(2,128)S(1)}, f32[2,2048]{1,0:T(2,128)S(1)}, u32[]{:S(2)}, u32[]{:S(2)}) collective-permute-start(f32[2,2048]{1,0:T(2,128)S(1)} %collective-permute-done.8), channel_id=1, source_target_pairs={{0,2},{2,4},{4,6},{6,8},{8,10},{10,12},{12,14},{14,0},{1,3},{3,5},... | collective-permute-start | bytes 49160 | tf_op jit(solution)/shard_map/ppermute | solution.py:95
  114.5 6.4 %collective-permute-start.10 = (f32[2,2048]{1,0:T(2,128)S(1)}, f32[2,2048]{1,0:T(2,128)S(1)}, u32[]{:S(2)}, u32[]{:S(2)}) collective-permute-start(f32[2,2048]{1,0:T(2,128)S(1)} %collective-permute-done.9), channel_id=1, source_target_pairs={{0,2},{2,4},{4,6},{6,8},{8,10},{10,12},{12,14},{14,0},{1,3},{3,5},... | collective-permute-start | bytes 49160 | tf_op jit(solution)/shard_map/ppermute | solution.py:95
  127.7 31.6 %copy-start.4 = (f32[16,16]{1,0:T(8,128)S(1)}, f32[16,16]{1,0:T(8,128)}, u32[]{:S(2)}) copy-start(f32[16,16]{1,0:T(8,128)} %param.11) | copy-start | bytes 3076
  162.0 29.4 %all-to-all-start.1 = ((f32[8,2,16384]{2,1,0:T(2,128)}), f32[8,2,16384]{2,1,0:T(2,128)S(1)}, u32[]{:S(2)}, u32[]{:S(2)}) async-start(f32[8,2,16384]{2,1,0:T(2,128)} %all_to_all.30), calls=%async_computation.1 | async-start | bytes 2097152 | tf_op jit(solution)/shard_map/all_to_all | solution.py:113
